TPU v7x, 32 devices: a whole 2x2x4 slice. The times are simulated.
32 devices in a mesh: groups: 2 (over y), tensor: 4 (over z), section: 4 (over x, core).
Axes of the slice: x: 2, y: 2, z: 4, core: 2. Of those that a mesh axis runs over, the one named last changes fastest.
Arguments:
- inputs: bfloat16 [4, 64, 8192], P('groups', None, 'tensor'), parts along dimension 0, may hold values from -6 to 6
- gains: bfloat16 [4, 8192], P('section'), may hold values from 0.099609375 to 1.8984375
- keep_mask: int32 [4, 128, 128], P('section', 'tensor'), may hold values from 0 to 1, as said below
- block_values: bfloat16 [4, 12288, 4096], P('section', 'tensor'), may hold values from -0.09375 to 0.09375
- head: bfloat16 [32000, 8192], P(('tensor', 'section')), may hold values from -30 to 30
- targets: int32 [4, 64], P('groups'), parts along dimension 0, may hold values from 0 to 31999
Outputs:
- token_loss: float32 [4, 64], P('groups'), parts along dimension 0
- mean_loss: float32 [2], P('groups'), parts along dimension 0
There are 2 independent parts, one for each index of `groups`. A program takes and returns all parts, laid end to end along the dimension named above; an argument that names none is the same for every part. Nothing has to cross between parts.
Inputs may be any that keep to these rules, and one draw needn't show every extreme that they name: `keep_mask`: in each section, band t (block rows t * 32 to (t + 1) * 32 - 1) keeps between 1024 and 3072 blocks, and some band of each section keeps exactly 3072. List slots past a band's count of kept blocks are not read.
All inputs are finite; a program needn't handle non-finite values.
Results may differ from a plain program's by a relative error of at most 0.0044.
The roundings to bfloat16 on the way count: a program that leaves them out, or rounds other values in their place, can miss the bound.
Values may be sent and summed in bfloat16 or wider, within the bound.
A program may use at most 320 MiB of HBM per device.

v0:
```python
import jax
import jax.numpy as jnp
from jax import lax
from jax.sharding import PartitionSpec as P

D = 8192
BLK = 64


epsilon = 1e-05


def shifted(block, axis, distance):
    devices = range(lax.axis_size(axis))
    route = [(i - distance, i) for i in devices if i - distance in devices]
    return lax.ppermute(block, axis, route)


def from_root(block, axis, source):
    block = jnp.where(lax.axis_index(axis) == source, block, jnp.zeros_like(block))
    return lax.psum(block, axis)


def joined(value, axis, combine):
    everything = jax.tree.map(lambda part: lax.all_gather(part, axis), value)
    leading = jax.tree.map(lambda part: part[0], everything)

    def turn(k, so_far):
        return combine(so_far, jax.tree.map(lambda part: part[k], everything))

    return lax.fori_loop(1, lax.axis_size(axis), turn, leading)


def merge_parts(earlier, later):
    top = jnp.maximum(earlier[0], later[0])
    total = earlier[1] * jnp.exp(earlier[0] - top) + later[1] * jnp.exp(later[0] - top)
    return (top, total, earlier[2] + later[2])


def on_device(inputs, gains, keep_mask, block_values, head, targets):
    section_count = lax.axis_size("section")
    tensor_index = lax.axis_index("tensor")
    section_index = lax.axis_index("section")
    micro_count, row_count, local_width = inputs.shape
    band_rows, block_count = (keep_mask.shape[1], keep_mask.shape[2])
    flat_mask = keep_mask[0].reshape(-1)
    slots = jnp.clip(jnp.cumsum(flat_mask, dtype=jnp.int32) - 1, 0, block_values.shape[1] - 1)
    picked = block_values[0][slots] * flat_mask[:, None].astype(jnp.bfloat16)
    panel = (
        picked.reshape(band_rows, block_count, BLK, BLK)
        .transpose(0, 2, 1, 3)
        .reshape(band_rows * BLK, D)
    )
    gain_row = gains[0]
    column_panel = lax.all_to_all(panel, "tensor", split_axis=1, concat_axis=0, tiled=True)
    timesteps = micro_count + section_count - 1
    incoming = jnp.zeros((row_count, local_width), jnp.bfloat16)
    finished = [None] * micro_count
    for moment in range(timesteps):
        current = jnp.where(section_index == 0, inputs[min(moment, micro_count - 1)], incoming)
        apply_widened = lax.all_gather(current, "tensor", axis=1, tiled=True).astype(jnp.float32)
        scaled = (apply_widened * gain_row.astype(jnp.float32)).astype(jnp.bfloat16)
        projected = jnp.dot(scaled, column_panel, preferred_element_type=jnp.float32)
        projected, apply_sumsq = (projected, jnp.sum(apply_widened * apply_widened, axis=1))
        update = projected * lax.rsqrt(apply_sumsq[:, None] / D + epsilon)
        outgoing = (current.astype(jnp.float32) + update).astype(jnp.bfloat16)
        done_index = moment - (section_count - 1)
        if 0 <= done_index < micro_count:
            finished[done_index] = outgoing
        if moment < timesteps - 1:
            incoming = shifted(outgoing, "section", 1)
    final_rows = jnp.stack(finished).reshape(micro_count * row_count, local_width)
    vocab_rows = head.shape[0]
    relayed = from_root(final_rows, "section", section_count - 1)
    portion = lax.all_gather(relayed, "tensor", axis=1, tiled=True)
    raw_logits = lax.dot_general(
        portion, head, (((1,), (1,)), ((), ())), preferred_element_type=jnp.float32
    )
    widened = portion.astype(jnp.float32)
    raw_logits, final_sumsq = (raw_logits, jnp.sum(widened * widened, axis=1))
    logits = raw_logits * lax.rsqrt(final_sumsq[:, None] / D + epsilon)
    vocab_start = (tensor_index * section_count + section_index) * vocab_rows
    local_ids = targets.reshape(-1) - vocab_start
    matches = jnp.arange(vocab_rows, dtype=jnp.int32)[None, :] == local_ids[:, None]
    target_logit = jnp.sum(jnp.where(matches, logits, 0.0), axis=1)
    local_top = jnp.max(logits, axis=1)
    local_total = jnp.sum(jnp.exp(logits - local_top[:, None]), axis=1)
    top, total, chosen = joined(
        (local_top, local_total, target_logit), ("tensor", "section"), merge_parts
    )
    token_loss = (top + jnp.log(total) - chosen).reshape(micro_count, row_count)
    mean_loss = jnp.mean(token_loss).reshape(1)
    return (token_loss, mean_loss)


def solution(mesh):
    placed = (
        P("groups", None, "tensor"),
        P("section", None),
        P("section", "tensor", None),
        P("section", "tensor", None),
        P(("tensor", "section"), None),
        P("groups", None),
    )
    return jax.shard_map(
        on_device,
        mesh=mesh,
        in_specs=placed,
        out_specs=(P("groups", None), P("groups")),
        check_vma=False,
    )
```

profile of v0, /device:TPU:0, one launch (start us, length us, event | category | flops | bytes accessed | tf_op | source)
XLA Modules:
  0.0 1553.5 jit_solution(10972753995354582155)
XLA Ops:
  7.2 0.7 bitcast_convert_fusion
  7.9 1.0 reduce-window.9
  8.9 0.1 slice.40
  9.0 0.1 reduce-window.12
  9.0 0.1 slice_reduce_fusion
  9.1 0.1 add_clamp_fusion
  9.3 67.2 %gather_fusion = bf16[4096,4096]{1,0:T(8,128)(2,1)} fusion(bf16[3072,4096]{1,0:T(8,128)(2,1)} %bitcast.77, s32[4096]{0:T(1024)S(1)} %broadcast_clamp_fusion), kind=kCustom, calls=%fused_computation | custom fusion | bytes 67125248 | tf_op jit(solution)/shard_map/gather | solution.py:48
  76.4 41.0 %copy.11 = bf16[4096,4096]{0,1:T(8,128)(2,1)} copy(bf16[4096,4096]{1,0:T(8,128)(2,1)} %gather_fusion) | data formatting | bytes 67108864 | tf_op jit(solution)/shard_map/gather | solution.py:48
  117.4 23.1 %copy.14 = bf16[512,8,32,128]{3,2,1,0:T(8,128)(2,1)} copy(bf16[512,8,32,128]{3,1,2,0:T(8,128)(2,1)} %bitcast.84) | data formatting | bytes 67108864
  140.5 23.1 %multiply_bitcast_fusion = bf16[32,64,128,64]{2,0,3,1:T(8,128)(2,1)} fusion(bf16[32,128,64,64]{1,0,3,2:T(8,128)(2,1)} %bitcast.83, bf16[32,128]{1,0:T(8,128)(2,1)S(1)} %bitcast_convert_fusion), kind=kLoop, calls=%fused_computation.11 | loop fusion | flops 16777216 | bytes 67117056 | tf_op jit(solution)/shard_map/transpose | solution.py:51
  163.6 110.4 %copy.12 = bf16[32,64,128,64]{1,0,3,2:T(8,128)(2,1)} copy(bf16[32,64,128,64]{2,0,3,1:T(8,128)(2,1)} %multiply_bitcast_fusion) | data formatting | bytes 67108864 | tf_op jit(solution)/shard_map/transpose | solution.py:51
  274.0 90.3 %all_to_all.14 = bf16[2048,4,2048]{0,2,1:T(8,128)(2,1)} reshape(bf16[32,64,128,64]{1,0,3,2:T(8,128)(2,1)} %copy.12) | data formatting | bytes 67108864 | tf_op jit(solution)/shard_map/all_to_all | solution.py:55
  364.4 9.8 all-to-all-start
  374.2 0.0 all-gather.24.cloned.1.call-start
  374.3 0.7 slice_select_fusion
  375.0 0.0 all-gather.24.cloned.1.call-update
  375.0 0.2 all-gather.14.cloned.1.call-start
  375.3 210.5 %all-gather.24.cloned.1.call-done = bf16[1,64,8192]{2,1,0:T(8,128)(2,1)} async-done(((bf16[1,64,2048]{2,1,0:T(8,128)(2,1)}), bf16[1,64,8192]{2,1,0:T(8,128)(2,1)}) %all-gather.24.cloned.1.call-update) | async-done | bytes 1048592 | tf_op jit(solution)/shard_map/all_gather | solution.py:61
  585.8 1.5 fusion.18
  587.4 527.8 %all-to-all-done = bf16[2048,4,2048]{0,2,1:T(8,128)(2,1)} async-done(((bf16[2048,4,2048]{0,2,1:T(8,128)(2,1)}), bf16[2048,4,2048]{0,2,1:T(8,128)(2,1)}, u32[]{:S(2)}, u32[]{:S(2)}) %all-to-all-start) | async-done | bytes 33554464 | tf_op jit(solution)/shard_map/all_to_all | solution.py:55
  1115.1 42.8 %copy.13 = bf16[4,2048,2048]{2,1,0:T(8,128)(2,1)} copy(bf16[4,2048,2048]{1,2,0:T(8,128)(2,1)} %bitcast.12) | data formatting | bytes 67108864 | tf_op jit(solution)/shard_map/all_to_all | solution.py:55
  1157.9 13.7 fusion.8
  1171.7 1.3 collective-permute-start
  1173.0 1.1 collective-permute-done
  1174.1 0.7 bitcast_select_fusion.3
  1174.8 0.0 all-gather.16.cloned.1.call-start
  1174.9 32.4 %all-gather.14.cloned.1.call-done = bf16[64,8192]{1,0:T(8,128)(2,1)} async-done(((bf16[64,2048]{1,0:T(8,128)(2,1)}), bf16[64,8192]{1,0:T(8,128)(2,1)}) %all-gather.14.cloned.1.call-update) | async-done | bytes 1048592 | tf_op jit(solution)/shard_map/all_gather | solution.py:61
  1207.3 1.5 fusion.10
  1208.9 16.8 %add_convert_fusion.3 = bf16[64,2048]{1,0:T(8,128)(2,1)S(1)} fusion(bf16[64,2048]{1,0:T(8,128)(2,1)} %bitcast_select_fusion.3, f32[64]{0:T(128)S(1)} %add_rsqrt_fusion.4, bf16[8192,2048]{1,0:T(8,128)(2,1)} %bitcast.79, bf16[64,8192]{1,0:T(8,128)(2,1)} %all-gather.14.cloned.1.call-done, f32[8192]{0:T(1024)S(1)} %bitcast.86), kind=kOutput, calls=%fused_computation.54 | convolution fusion | flops 2149580800 | bytes 35160320 | tf_op jit(solution)/shard_map/dot_general | solution.py:63
  1225.7 1.6 collective-permute-start.1
  1227.3 1.1 collective-permute-done.1
  1228.4 0.7 bitcast_select_fusion.2
  1229.2 0.3 all-gather.18.cloned.1.call-start
  1229.4 32.3 %all-gather.16.cloned.1.call-done = bf16[64,8192]{1,0:T(8,128)(2,1)} async-done(((bf16[64,2048]{1,0:T(8,128)(2,1)}), bf16[64,8192]{1,0:T(8,128)(2,1)}) %all-gather.16.cloned.1.call-update) | async-done | bytes 1048592 | tf_op jit(solution)/shard_map/all_gather | solution.py:61
  1261.7 1.5 fusion.12
  1263.2 16.8 %add_convert_fusion.2 = bf16[64,2048]{1,0:T(8,128)(2,1)S(1)} fusion(bf16[64,2048]{1,0:T(8,128)(2,1)} %bitcast_select_fusion.2, f32[64]{0:T(128)S(1)} %add_rsqrt_fusion.3, bf16[8192,2048]{1,0:T(8,128)(2,1)} %bitcast.80, bf16[64,8192]{1,0:T(8,128)(2,1)} %all-gather.16.cloned.1.call-done, f32[8192]{0:T(1024)S(1)} %bitcast.87), kind=kOutput, calls=%fused_computation.53 | convolution fusion | flops 2149580800 | bytes 35160320 | tf_op jit(solution)/shard_map/dot_general | solution.py:63
  1280.0 1.6 collective-permute-start.2
  1281.7 1.1 collective-permute-done.2
  1282.8 0.7 bitcast_select_fusion.1
  1283.5 0.0 all-gather.20.cloned.1.call-start
  1283.6 32.5 %all-gather.18.cloned.1.call-done = bf16[64,8192]{1,0:T(8,128)(2,1)} async-done(((bf16[64,2048]{1,0:T(8,128)(2,1)}), bf16[64,8192]{1,0:T(8,128)(2,1)}) %all-gather.18.cloned.1.call-update) | async-done | bytes 1048592 | tf_op jit(solution)/shard_map/all_gather | solution.py:61
  1316.1 1.5 fusion.14
  1317.6 16.8 %add_convert_fusion.1 = bf16[64,2048]{1,0:T(8,128)(2,1)S(1)} fusion(bf16[64,2048]{1,0:T(8,128)(2,1)} %bitcast_select_fusion.1, f32[64]{0:T(128)S(1)} %add_rsqrt_fusion.2, bf16[8192,2048]{1,0:T(8,128)(2,1)} %bitcast.81, bf16[64,8192]{1,0:T(8,128)(2,1)} %all-gather.18.cloned.1.call-done, f32[8192]{0:T(1024)S(1)} %bitcast.88), kind=kOutput, calls=%fused_computation.52 | convolution fusion | flops 2149580800 | bytes 35160320 | tf_op jit(solution)/shard_map/dot_general | solution.py:63
  1334.4 1.6 collective-permute-start.3
  1336.0 1.1 collective-permute-done.3
  1337.2 0.7 bitcast_select_fusion
  1337.9 0.3 all-reduce.2.cloned.1.call-start
  1338.2 32.2 %all-gather.20.cloned.1.call-done = bf16[64,8192]{1,0:T(8,128)(2,1)} async-done(((bf16[64,2048]{1,0:T(8,128)(2,1)}), bf16[64,8192]{1,0:T(8,128)(2,1)}) %all-gather.20.cloned.1.call-update) | async-done | bytes 1048592 | tf_op jit(solution)/shard_map/all_gather | solution.py:61
  1370.4 1.5 fusion.16
  1372.0 16.8 %fusion.30 = bf16[1,64,2048]{2,1,0:T(8,128)(2,1)S(1)} fusion(bf16[64,2048]{1,0:T(8,128)(2,1)} %bitcast_select_fusion, f32[64]{0:T(128)S(1)} %add_rsqrt_fusion.1, bf16[8192,2048]{1,0:T(8,128)(2,1)} %bitcast.82, bf16[64,8192]{1,0:T(8,128)(2,1)} %all-gather.20.cloned.1.call-done, f32[8192]{0:T(1024)S(1)} %bitcast.89), kind=kOutput, calls=%fused_computation.55 | convolution fusion | flops 2149580800 | bytes 35160320 | tf_op jit(solution)/shard_map/dot_general | solution.py:63
  1388.8 0.9 maximum_select_fusion
  1389.7 0.0 all-gather.22.cloned.1.call-start
  1389.7 32.8 %all-reduce.2.cloned.1.call-done = bf16[128,2048]{1,0:T(8,128)(2,1)} async-done(((bf16[128,2048]{1,0:T(8,128)(2,1)}), bf16[128,2048]{1,0:T(8,128)(2,1)}) %all-reduce.2.cloned.1.call-update) | async-done | bytes 524304 | tf_op jit(solution)/shard_map/psum | solution.py:21
  1422.6 0.1 sub.53
  1422.7 47.4 %all-gather.22.cloned.1.call-done = bf16[128,8192]{1,0:T(8,128)(2,1)} async-done(((bf16[128,2048]{1,0:T(8,128)(2,1)}), bf16[128,8192]{1,0:T(8,128)(2,1)}) %all-gather.22.cloned.1.call-update) | async-done | bytes 2097168 | tf_op jit(solution)/shard_map/all_gather | solution.py:75
  1470.1 2.1 multiply_reduce_fusion
  1472.2 15.0 fusion.41
  1487.2 19.0 %all-gather.4 = f32[16,1,128]{2,1,0:T(1,128)S(1)} all-gather(f32[1,1,128]{2,1,0:T(1,128)S(1)} %bitcast.98), channel_id=3, replica_groups=mesh['groups'=2,'tensor'=4,'section'=4] {'tensor','section'}, dimensions={0}, use_global_device_ids=true | all-gather | bytes 8704 | tf_op jit(solution)/shard_map/all_gather | solution.py:25
  1506.3 0.3 select_reduce_fusion
  1506.5 17.3 %all-gather.5 = f32[16,1,128]{2,1,0:T(1,128)S(1)} all-gather(f32[1,1,128]{2,1,0:T(1,128)S(1)} %bitcast.100), channel_id=4, replica_groups=mesh['groups'=2,'tensor'=4,'section'=4] {'tensor','section'}, dimensions={0}, use_global_device_ids=true | all-gather | bytes 8704 | tf_op jit(solution)/shard_map/all_gather | solution.py:25
  1523.8 18.7 %all-gather.6 = f32[16,1,128]{2,1,0:T(1,128)S(1)} all-gather(f32[1,1,128]{2,1,0:T(1,128)S(1)} %bitcast.99), channel_id=5, replica_groups=mesh['groups'=2,'tensor'=4,'section'=4] {'tensor','section'}, dimensions={0}, use_global_device_ids=true | all-gather | bytes 8704 | tf_op jit(solution)/shard_map/all_gather | solution.py:25
  1542.5 0.7 while.19
  1543.2 0.6 fusion.40
  1543.8 0.6 reshape.147
  (44 shorter events, 0.7 us)
Async XLA Ops:
  364.3 9.9 copy-start.1
  364.3 10.9 copy-start.3
  364.4 750.8 %all-to-all-start = ((bf16[2048,4,2048]{0,2,1:T(8,128)(2,1)}), bf16[2048,4,2048]{0,2,1:T(8,128)(2,1)}, u32[]{:S(2)}, u32[]{:S(2)}) async-start(bf16[2048,4,2048]{0,2,1:T(8,128)(2,1)} %all_to_all.14), calls=%async_computation | async-start | bytes 67108864 | tf_op jit(solution)/shard_map/all_to_all | solution.py:55
  374.2 211.6 %all-gather.24.cloned.1.call-start = ((), (), s32[]{:S(2)}) async-start(), calls=%async_computation.7 | async-start | bytes 1310720 | tf_op jit(solution)/shard_map/all_gather | solution.py:61
  375.0 832.3 %all-gather.14.cloned.1.call-start = ((), (), s32[]{:S(2)}) async-start(), calls=%async_computation.1 | async-start | bytes 1310720 | tf_op jit(solution)/shard_map/all_gather | solution.py:61
  1115.1 42.8 %copy-start = (bf16[1,64,8192]{2,1,0:T(8,128)(2,1)S(1)}, bf16[1,64,8192]{2,1,0:T(8,128)(2,1)}, u32[]{:S(2)}) copy-start(bf16[1,64,8192]{2,1,0:T(8,128)(2,1)} %all-gather.24.cloned.1.call-done) | copy-start | bytes 3145732
  1115.1 42.8 %copy-start.2 = (bf16[1,64,2048]{2,1,0:T(8,128)(2,1)S(1)}, bf16[1,64,2048]{2,1,0:T(8,128)(2,1)}, u32[]{:S(2)}) copy-start(bf16[1,64,2048]{2,1,0:T(8,128)(2,1)} %slice_select_fusion) | copy-start | bytes 786436
  1171.7 2.4 collective-permute-start
  1174.8 86.8 %all-gather.16.cloned.1.call-start = ((), (), s32[]{:S(2)}) async-start(), calls=%async_computation.2 | async-start | bytes 1310720 | tf_op jit(solution)/shard_map/all_gather | solution.py:61
  1225.7 2.8 collective-permute-start.1
  1229.2 86.9 %all-gather.18.cloned.1.call-start = ((), (), s32[]{:S(2)}) async-start(), calls=%async_computation.3 | async-start | bytes 1310720 | tf_op jit(solution)/shard_map/all_gather | solution.py:61
  1280.0 2.8 collective-permute-start.2
  1283.5 86.9 %all-gather.20.cloned.1.call-start = ((), (), s32[]{:S(2)}) async-start(), calls=%async_computation.4 | async-start | bytes 1310720 | tf_op jit(solution)/shard_map/all_gather | solution.py:61
  1334.4 88.2 %copy-start.4 = (s32[2,64]{1,0:T(2,128)S(1)}, s32[2,64]{1,0:T(2,128)}, u32[]{:S(2)}) copy-start(s32[2,64]{1,0:T(2,128)} %param.13) | copy-start | bytes 1540
  1334.4 2.8 collective-permute-start.3
  1337.9 84.6 %all-reduce.2.cloned.1.call-start = ((), (), s32[]{:S(2)}) async-start(), calls=%async_computation.5 | async-start | bytes 1048576 | tf_op jit(solution)/shard_map/psum | solution.py:21
  1389.7 80.4 %all-gather.22.cloned.1.call-start = ((), (), s32[]{:S(2)}) async-start(), calls=%async_computation.6 | async-start | bytes 2621440 | tf_op jit(solution)/shard_map/all_gather | solution.py:75
Sparse Core Ops, SparseCore 0:
  376.6 209.1 all-gather.23
  1175.0 32.3 all-gather.13
  1229.3 32.3 all-gather.15
  1283.7 32.3 all-gather.17
  1338.0 32.3 all-gather.19
  1389.8 32.6 all-reduce.1
  1424.1 45.9 all-gather.21
where the time goes:
time: 1570 us; the launch traced here: 1550 us
  waiting for transfers between devices  952 us (61%)
  local copies, waits for them, and re-layouts  376 us (24%)
  matrix products  95.9 us (6%)
  blocking collectives  55 us (4%)
  other arithmetic  40.6 us (3%)
  starting transfers between devices  16.9 us (1%)
  between operations  16.6 us (1%)
    all_to_all x1, waiting for transfers between devices, on_device(): lax.all_to_all(panel, 'tensor', split_axis=1, concat_axis=0, tiled=True)  528 us
    all_gather x5, waiting for transfers between devices, on_device(): lax.all_gather(current, 'tensor', axis=1, tiled=True).astype(jnp.float32)  340 us
    all_to_all x2, local copies, waits for them, and re-layouts, on_device(): lax.all_to_all(panel, 'tensor', split_axis=1, concat_axis=0, tiled=True)  133 us
    transpose x1, local copies, waits for them, and re-layouts, on_device(): panel = picked.reshape(band_rows, block_count, BLK, BLK).transpose(0, 2,...  110 us
    gather x2, local copies, waits for them, and re-layouts, on_device(): picked = block_values[0][slots] * flat_mask[:, None].astype(jnp.bfloat16)  108 us
    dot_general x5, matrix products, on_device(): jnp.dot(scaled, column_panel, preferred_element_type=jnp.float32)  80.9 us
    all_gather x3, blocking collectives, joined(): everything = jax.tree.map(lambda part: lax.all_gather(part, axis), value)  55 us
    all_gather x1, waiting for transfers between devices, on_device(): portion = lax.all_gather(relayed, 'tensor', axis=1, tiled=True)  47.4 us
  transfers between devices with their start and end apart: 12, of which 12 were waited for; matrix products, arithmetic and copies ran while one was open for 0% of the time, Pallas kernels for 0%

commit v1 on v0

v1 whole, which is shorter than its diff:
```python
import jax
import jax.numpy as jnp
from jax import lax
from jax.experimental import pallas as pl
from jax.experimental.pallas import tpu as pltpu
from jax.sharding import PartitionSpec as P

D = 8192
BLK = 64
PAIR = 2 * BLK
HALF = BLK // 2

epsilon = 1e-05


def shifted(block, axis, distance):
    devices = range(lax.axis_size(axis))
    route = [(i - distance, i) for i in devices if i - distance in devices]
    return lax.ppermute(block, axis, route)


def build_body(block_count, index_ref, start_ref, window_ref, panel_ref):
    row = pl.program_id(0)
    start = start_ref[row]
    for column in range(block_count):
        slot = index_ref[row * block_count + column]
        near = jnp.clip(slot - start, 0, window_ref.shape[0] - 1)
        keep = jnp.where(slot >= 0, 1.0, 0.0).astype(jnp.float32)
        factor = jnp.full((HALF, PAIR), keep, jnp.float32).astype(jnp.bfloat16)
        panel_ref[:, column * PAIR : (column + 1) * PAIR] = window_ref[near] * factor


def build_panel(mask, values):
    band_rows, block_count = mask.shape
    slot_count = values.shape[0]
    running = jnp.cumsum(mask.reshape(-1), dtype=jnp.int32)
    slots = jnp.clip(running - 1, 0, slot_count - 1)
    index = jnp.where(mask.reshape(-1) > 0, slots, -1)
    before = running.reshape(band_rows, block_count)[:, 0] - mask[:, 0]
    window = min(block_count, slot_count)
    starts = jnp.clip(before, 0, slot_count - window).astype(jnp.int32)
    lists = values.reshape(slot_count, HALF, PAIR)
    spec = pltpu.PrefetchScalarGridSpec(
        num_scalar_prefetch=2,
        grid=(band_rows,),
        in_specs=[
            pl.BlockSpec(
                (pl.Element(window), pl.Element(HALF), pl.Element(PAIR)),
                lambda r, index_ref, start_ref: (start_ref[r], 0, 0),
            )
        ],
        out_specs=pl.BlockSpec((HALF, block_count * PAIR), lambda r, *_: (r, 0)),
    )

    def body(*refs):
        build_body(block_count, *refs)

    return pl.pallas_call(
        body,
        grid_spec=spec,
        out_shape=jax.ShapeDtypeStruct((band_rows * HALF, block_count * PAIR), jnp.bfloat16),
        compiler_params=pltpu.CompilerParams(
            dimension_semantics=("arbitrary",), vmem_limit_bytes=40 << 20
        ),
    )(index, starts, lists)


def joined_loss(logits_top, total, chosen):
    stacked = jnp.stack([logits_top, total, chosen])
    everything = lax.all_gather(stacked, ("tensor", "section"))
    tops = everything[:, 0]
    top = jnp.max(tops, axis=0)
    total = jnp.sum(everything[:, 1] * jnp.exp(tops - top[None, :]), axis=0)
    return top + jnp.log(total) - jnp.sum(everything[:, 2], axis=0)


def on_device(inputs, gains, keep_mask, block_values, head, targets):
    section_count = lax.axis_size("section")
    tensor_index = lax.axis_index("tensor")
    section_index = lax.axis_index("section")
    micro_count, row_count, local_width = inputs.shape
    rows = micro_count * row_count
    panel = build_panel(keep_mask[0], block_values[0])
    gain = lax.dynamic_slice(gains[0], (tensor_index * local_width,), (local_width,))
    gain = gain.astype(jnp.float32)
    own = inputs.reshape(rows, local_width)
    incoming = own
    low = (jnp.arange(PAIR) < BLK)[None, None, :]
    for moment in range(section_count):
        current = jnp.where(section_index == 0, own, incoming) if moment else own
        wide = current.astype(jnp.float32)
        sumsq = lax.psum(jnp.sum(wide * wide, axis=1), "tensor")
        scaled = (wide * gain).astype(jnp.bfloat16)
        split = scaled.reshape(rows, local_width // 2, 2).transpose(2, 0, 1)
        both = jnp.dot(
            split.reshape(2 * rows, local_width // 2), panel, preferred_element_type=jnp.float32
        ).reshape(2, rows, D // BLK, PAIR)
        partial = (both[0, :, :, :BLK] + both[1, :, :, BLK:]).reshape(rows, D)
        product = lax.psum_scatter(partial, "tensor", scatter_dimension=1, tiled=True)
        update = product * lax.rsqrt(sumsq[:, None] / D + epsilon)
        outgoing = (wide + update).astype(jnp.bfloat16)
        if moment < section_count - 1:
            incoming = shifted(outgoing, "section", 1)
    vocab_rows = head.shape[0]
    final = jnp.where(section_index == section_count - 1, outgoing, jnp.zeros_like(outgoing))
    relayed = lax.psum(final, "section")
    portion = lax.all_gather(relayed, "tensor", axis=1, tiled=True)
    raw_logits = lax.dot_general(
        portion, head, (((1,), (1,)), ((), ())), preferred_element_type=jnp.float32
    )
    widened = portion.astype(jnp.float32)
    final_sumsq = jnp.sum(widened * widened, axis=1)
    logits = raw_logits * lax.rsqrt(final_sumsq[:, None] / D + epsilon)
    vocab_start = (tensor_index * section_count + section_index) * vocab_rows
    local_ids = targets.reshape(-1) - vocab_start
    matches = jnp.arange(vocab_rows, dtype=jnp.int32)[None, :] == local_ids[:, None]
    target_logit = jnp.sum(jnp.where(matches, logits, 0.0), axis=1)
    local_top = jnp.max(logits, axis=1)
    local_total = jnp.sum(jnp.exp(logits - local_top[:, None]), axis=1)
    losses = joined_loss(local_top, local_total, target_logit)
    token_loss = losses.reshape(micro_count, row_count)
    mean_loss = jnp.mean(token_loss).reshape(1)
    return (token_loss, mean_loss)


def solution(mesh):
    placed = (
        P("groups", None, "tensor"),
        P("section", None),
        P("section", "tensor", None),
        P("section", "tensor", None),
        P(("tensor", "section"), None),
        P("groups", None),
    )
    return jax.shard_map(
        on_device,
        mesh=mesh,
        in_specs=placed,
        out_specs=(P("groups", None), P("groups")),
        check_vma=False,
    )
```

time: 1570 us -> 745 us (0.47)
  waiting for transfers between devices: 952 us -> 372 us
  local copies, waits for them, and re-layouts: 376 us -> 95.3 us
  Pallas kernels: 0 us -> 41.4 us
    all_to_all x1 -> x0, waiting for transfers between devices: 528 us -> none  [on_device(): lax.all_to_all(panel, 'tensor', split_axis=1, concat_axis=0, tiled=True)]
    all_gather x5 -> x0, waiting for transfers between devices: 340 us -> none  [on_device(): lax.all_gather(current, 'tensor', axis=1, tiled=True).astype(jnp.float32)]
    reduce_scatter x0 -> x4, waiting for transfers between devices: none -> 286 us  [on_device(): lax.psum_scatter(partial, 'tensor', scatter_dimension=1, tiled=True)]
    all_to_all x2 -> x0, local copies, waits for them, and re-layouts: 133 us -> none  [on_device(): lax.all_to_all(panel, 'tensor', split_axis=1, concat_axis=0, tiled=True)]
    transpose x1 -> x0, local copies, waits for them, and re-layouts: 110 us -> none  [on_device(): panel = picked.reshape(band_rows, block_count, BLK, BLK).transpose(0, 2,...]
    gather x2 -> x0, local copies, waits for them, and re-layouts: 108 us -> none  [on_device(): picked = block_values[0][slots] * flat_mask[:, None].astype(jnp.bfloat16)]
    psum x0 -> x4, blocking collectives: none -> 46.8 us  [on_device(): sumsq = lax.psum(jnp.sum(wide * wide, axis=1), 'tensor')]
    dot_general x0 -> x1, local copies, waits for them, and re-layouts: none -> 44.1 us  [on_device(): jnp.dot(split.reshape(2 * rows, local_width // 2), panel, preferred_eleme...]
  transfers between devices with their start and end apart: 12 -> 9, of which waited for: 12 -> 9; matrix products, arithmetic and copies ran while one was open for 0% -> 0% of each run, Pallas kernels for 0% -> 0%
where the time goes in v1:
time: 745 us; the launch traced here: 741 us
  waiting for transfers between devices  372 us (50%)
  matrix products  98.9 us (13%)
  local copies, waits for them, and re-layouts  95.3 us (13%)
  blocking collectives  66 us (9%)
  other arithmetic  46.1 us (6%)
  Pallas kernels  41.4 us (6%)
  between operations  16.1 us (2%)
    reduce_scatter x4, waiting for transfers between devices, on_device(): lax.psum_scatter(partial, 'tensor', scatter_dimension=1, tiled=True)  286 us
    dot_general x4, matrix products, on_device(): jnp.dot(split.reshape(2 * rows, local_width // 2), panel, preferred_eleme...  83.8 us
    all_gather x1, waiting for transfers between devices, on_device(): portion = lax.all_gather(relayed, 'tensor', axis=1, tiled=True)  47.3 us
    psum x4, blocking collectives, on_device(): sumsq = lax.psum(jnp.sum(wide * wide, axis=1), 'tensor')  46.8 us
    dot_general x1, local copies, waits for them, and re-layouts, on_device(): jnp.dot(split.reshape(2 * rows, local_width // 2), panel, preferred_eleme...  44.1 us
    pallas_call x1, Pallas kernels, build_panel(): pl.pallas_call(body, grid_spec=spec, out_shape=jax.ShapeDtypeStruct((band...  41.4 us
    psum x1, waiting for transfers between devices, on_device(): relayed = lax.psum(final, 'section')  33.8 us
    add x4, other arithmetic, on_device(): partial = (both[0, :, :, :BLK] + both[1, :, :, BLK:]).reshape(rows, D)  27.5 us
  transfers between devices with their start and end apart: 9, of which 9 were waited for; matrix products, arithmetic and copies ran while one was open for 0% of the time, Pallas kernels for 0%

profile of v1, /device:TPU:0, one launch (start us, length us, event | category | flops | bytes accessed | tf_op | source)
XLA Modules:
  0.0 741.4 jit_solution(17023254560618214008)
XLA Ops:
  7.2 1.0 reduce-window.9
  8.2 0.1 slice.61
  8.3 0.1 slice_reduce_fusion
  8.5 0.8 bitcast_select_fusion.3
  9.3 0.8 fusion.20.refs_1_
  10.1 22.4 %copy.78 = bf16[384,8,32,128]{3,2,1,0:T(8,128)(2,1)} copy(bf16[384,8,32,128]{3,1,2,0:T(8,128)(2,1)} %bitcast.71) | data formatting | bytes 50331648
  32.5 41.4 %shard_map.77 = bf16[1024,16384]{1,0:T(8,128)(2,1)} custom-call(s32[4096]{0:T(1024)S(1)} %get-tuple-element.14.refs_0_, s32[32]{0:T(128)S(1)} %fusion.20.refs_1_, bf16[3072,32,128]{2,1,0:T(8,128)(2,1)} %bitcast.66), custom_call_target="tpu_custom_call" | custom-call | tf_op jit(solution)/shard_map/pallas_call | solution.py:58
  73.9 44.1 %copy.76 = bf16[16384,1024]{1,0:T(8,128)(2,1)} copy(bf16[16384,1024]{0,1:T(8,128)(2,1)} %bitcast.65) | data formatting | bytes 67108864 | tf_op jit(solution)/shard_map/dot_general | solution.py:95
  117.9 0.5 broadcast.89
  118.5 1.4 fusion.22
  119.8 0.5 mul.102
  120.3 0.8 copy.47
  121.1 2.8 reshape.148
  123.9 3.6 fusion.9
  127.5 20.9 %fusion.17 = f32[2,128,128,128]{1,3,2,0:T(8,128)} fusion(bf16[128,128,1024,1]{2,1,0,3:T(8,128)(2,1)} %bitcast.67, bf16[2,128,1024,1]{1,0,2,3:T(2,128)(2,1)S(1)} %fusion.9), kind=kOutput, calls=%fused_computation.38 | convolution fusion | flops 8589934592 | bytes 50855936 | tf_op jit(solution)/shard_map/dot_general | solution.py:95
  148.4 6.9 slice_add_fusion.3
  155.3 5.6 copy.50
  161.0 0.2 multiply_reduce_fusion.1
  161.2 0.1 reduce_sum.93
  161.3 13.5 %psum.35 = f32[128]{0:T(128)S(1)} all-reduce(f32[128]{0:T(128)S(1)} %reduce_sum.93), channel_id=1, replica_groups=mesh['groups'=2,'tensor'=4,'section'=4] {'tensor'}, use_global_device_ids=true, to_apply=%region_4.5 | all-reduce | flops 128 | bytes 1024 | tf_op jit(solution)/shard_map/psum | solution.py:92
  174.8 65.8 %reduce-scatter.5.cloned.1.call-done = f32[128,2048]{1,0:T(8,128)} async-done(((f32[128,8192]{1,0:T(8,128)}), f32[128,2048]{1,0:T(8,128)}) %reduce-scatter.5.cloned.1.call-update) | async-done | bytes 1048592 | tf_op jit(solution)/shard_map/reduce_scatter | solution.py:99
  240.7 1.4 add_convert_fusion
  242.1 2.0 collective-permute-start
  244.1 1.3 collective-permute-done
  245.4 0.3 fusion.1
  245.7 0.1 fusion
  245.9 0.3 copy.51
  246.1 21.0 %fusion.15 = f32[2,128,128,128]{1,3,2,0:T(8,128)} fusion(bf16[128,128,1024,1]{2,1,0,3:T(8,128)(2,1)} %bitcast.68, bf16[2,128,1024,1]{1,0,2,3:T(2,128)(2,1)S(1)} %bitcast.77), kind=kOutput, calls=%fused_computation.36 | convolution fusion | flops 8589934592 | bytes 50855936 | tf_op jit(solution)/shard_map/dot_general | solution.py:95
  267.1 6.9 slice_add_fusion.2
  274.0 5.6 copy.54
  279.7 11.0 %psum.36 = f32[128]{0:T(128)S(1)} all-reduce(f32[128]{0:T(128)S(1)} %get-tuple-element.10), channel_id=1, replica_groups=mesh['groups'=2,'tensor'=4,'section'=4] {'tensor'}, use_global_device_ids=true, to_apply=%region_7.8 | all-reduce | flops 128 | bytes 1024 | tf_op jit(solution)/shard_map/psum | solution.py:92
  290.7 73.5 %reduce-scatter.7.cloned.1.call-done = f32[128,2048]{1,0:T(8,128)} async-done(((f32[128,8192]{1,0:T(8,128)}), f32[128,2048]{1,0:T(8,128)}) %reduce-scatter.7.cloned.1.call-update) | async-done | bytes 1048592 | tf_op jit(solution)/shard_map/reduce_scatter | solution.py:99
  364.2 1.4 fusion.2
  365.6 1.8 collective-permute-start.1
  367.4 1.5 collective-permute-done.1
  368.9 0.3 fusion.4
  369.2 0.1 fusion.3
  369.3 0.3 copy.55
  369.6 21.0 %fusion.13 = f32[2,128,128,128]{1,3,2,0:T(8,128)} fusion(bf16[128,128,1024,1]{2,1,0,3:T(8,128)(2,1)} %bitcast.69, bf16[2,128,1024,1]{1,0,2,3:T(2,128)(2,1)S(1)} %bitcast.78), kind=kOutput, calls=%fused_computation.34 | convolution fusion | flops 8589934592 | bytes 50855936 | tf_op jit(solution)/shard_map/dot_general | solution.py:95
  390.5 6.9 slice_add_fusion.1
  397.4 5.6 copy.58
  403.1 11.1 %psum.37 = f32[128]{0:T(128)S(1)} all-reduce(f32[128]{0:T(128)S(1)} %get-tuple-element.8), channel_id=1, replica_groups=mesh['groups'=2,'tensor'=4,'section'=4] {'tensor'}, use_global_device_ids=true, to_apply=%region_10.11 | all-reduce | flops 128 | bytes 1024 | tf_op jit(solution)/shard_map/psum | solution.py:92
  414.2 73.5 %reduce-scatter.9.cloned.1.call-done = f32[128,2048]{1,0:T(8,128)} async-done(((f32[128,8192]{1,0:T(8,128)}), f32[128,2048]{1,0:T(8,128)}) %reduce-scatter.9.cloned.1.call-update) | async-done | bytes 1048592 | tf_op jit(solution)/shard_map/reduce_scatter | solution.py:99
  487.7 1.4 fusion.5
  489.1 2.0 collective-permute-start.2
  491.2 1.3 collective-permute-done.2
  492.4 0.3 fusion.7
  492.7 0.1 fusion.6
  492.9 0.3 copy.59
  493.1 21.0 %fusion.11 = f32[2,128,128,128]{1,3,2,0:T(8,128)} fusion(bf16[128,128,1024,1]{2,1,0,3:T(8,128)(2,1)} %bitcast.70, bf16[2,128,1024,1]{1,0,2,3:T(2,128)(2,1)S(1)} %bitcast.76), kind=kOutput, calls=%fused_computation.32 | convolution fusion | flops 8589934592 | bytes 50855936 | tf_op jit(solution)/shard_map/dot_general | solution.py:95
  514.1 6.8 slice_add_fusion
  520.9 5.6 copy.62
  526.6 11.1 %psum.38 = f32[128]{0:T(128)S(1)} all-reduce(f32[128]{0:T(128)S(1)} %get-tuple-element.6), channel_id=1, replica_groups=mesh['groups'=2,'tensor'=4,'section'=4] {'tensor'}, use_global_device_ids=true, to_apply=%region_13.14 | all-reduce | flops 128 | bytes 1024 | tf_op jit(solution)/shard_map/psum | solution.py:92
  537.7 73.5 %reduce-scatter.11.cloned.1.call-done = f32[128,2048]{1,0:T(8,128)} async-done(((f32[128,8192]{1,0:T(8,128)}), f32[128,2048]{1,0:T(8,128)}) %reduce-scatter.11.cloned.1.call-update) | async-done | bytes 1048592 | tf_op jit(solution)/shard_map/reduce_scatter | solution.py:99
  611.2 2.3 fusion.10
  613.6 33.8 %all-reduce.2.cloned.1.call-done = bf16[128,2048]{1,0:T(8,128)(2,1)} async-done(((bf16[128,2048]{1,0:T(8,128)(2,1)}), bf16[128,2048]{1,0:T(8,128)(2,1)}) %all-reduce.2.cloned.1.call-update) | async-done | bytes 524304 | tf_op jit(solution)/shard_map/psum | solution.py:106
  647.4 0.1 sub.51
  647.5 47.3 %all-gather.4.cloned.1.call-done = bf16[128,8192]{1,0:T(8,128)(2,1)} async-done(((bf16[128,2048]{1,0:T(8,128)(2,1)}), bf16[128,8192]{1,0:T(8,128)(2,1)}) %all-gather.4.cloned.1.call-update) | async-done | bytes 2097168 | tf_op jit(solution)/shard_map/all_gather | solution.py:107
  694.8 2.1 multiply_reduce_fusion
  696.9 15.1 %fusion.24 = (f32[128]{0:T(128)S(1)}, f32[128,2000]{0,1:T(8,128)S(1)}) fusion(f32[128]{0:T(128)S(1)} %add_rsqrt_fusion, bf16[128,8192]{1,0:T(8,128)(2,1)} %all-gather.4.cloned.1.call-done, bf16[2000,8192]{1,0:T(8,128)(2,1)} %param.10), kind=kOutput, calls=%fused_computation.63 | convolution fusion | flops 4194816000 | bytes 35890176 | tf_op jit(solution)/shard_map/dot_general | solution.py:108
  712.0 0.3 exponential_reduce_fusion
  712.3 19.2 %all-gather.1 = f32[16,3,128]{2,1,0:T(4,128)S(1)} all-gather(f32[1,3,128]{2,1,0:T(4,128)S(1)} %maximum_bitcast_fusion), channel_id=2, replica_groups=mesh['groups'=2,'tensor'=4,'section'=4] {'tensor','section'}, dimensions={0}, use_global_device_ids=true | all-gather | bytes 26112 | tf_op jit(solution)/shard_map/all_gather | solution.py:70
  731.5 0.6 fusion.21
  732.2 0.6 sub.55
  (27 shorter events, 0.5 us)
Async XLA Ops:
  7.2 233.5 %reduce-scatter.5.cloned.1.call-start = ((), (), s32[]{:S(2)}) async-start(), calls=%async_computation.4 | async-start | bytes 5242880 | tf_op jit(solution)/shard_map/reduce_scatter | solution.py:99
  73.9 46.4 %copy-start = (bf16[2,64,2048]{2,1,0:T(8,128)(2,1)S(1)}, bf16[2,64,2048]{2,1,0:T(8,128)(2,1)}, u32[]{:S(2)}) copy-start(bf16[2,64,2048]{2,1,0:T(8,128)(2,1)} %param.6) | copy-start | bytes 1572868
  161.0 203.2 %reduce-scatter.7.cloned.1.call-start = ((), (), s32[]{:S(2)}) async-start(), calls=%async_computation.5 | async-start | bytes 5242880 | tf_op jit(solution)/shard_map/reduce_scatter | solution.py:99
  242.1 3.3 collective-permute-start
  279.6 208.1 %reduce-scatter.9.cloned.1.call-start = ((), (), s32[]{:S(2)}) async-start(), calls=%async_computation.6 | async-start | bytes 5242880 | tf_op jit(solution)/shard_map/reduce_scatter | solution.py:99
  365.6 3.3 collective-permute-start.1
  403.0 208.2 %reduce-scatter.11.cloned.1.call-start = ((), (), s32[]{:S(2)}) async-start(), calls=%async_computation.7 | async-start | bytes 5242880 | tf_op jit(solution)/shard_map/reduce_scatter | solution.py:99
  489.1 3.3 collective-permute-start.2
  514.1 133.3 %copy-start.1 = (s32[2,64]{1,0:T(2,128)S(1)}, s32[2,64]{1,0:T(2,128)}, u32[]{:S(2)}) copy-start(s32[2,64]{1,0:T(2,128)} %param.11) | copy-start | bytes 1540
  526.6 120.8 %all-reduce.2.cloned.1.call-start = ((), (), s32[]{:S(2)}) async-start(), calls=%async_computation.8 | async-start | bytes 1048576 | tf_op jit(solution)/shard_map/psum | solution.py:106
  613.5 81.3 %all-gather.4.cloned.1.call-start = ((), (), s32[]{:S(2)}) async-start(), calls=%async_computation.9 | async-start | bytes 2621440 | tf_op jit(solution)/shard_map/all_gather | solution.py:107
Sparse Core Ops, SparseCore 0:
  161.1 79.5 reduce-scatter.4
  279.7 84.3 reduce-scatter.6
  403.2 84.5 reduce-scatter.8
  526.7 84.5 reduce-scatter.10
  613.6 33.7 all-reduce.1
  648.8 45.9 all-gather.3
